TPU v7x, 32 devices: a whole 2x2x4 slice. The times are simulated.
32 devices in a mesh: pt: 8 (over z, y), tm: 4 (over x, core).
Axes of the slice: x: 2, y: 2, z: 4, core: 2. Of those that a mesh axis runs over, the one named last changes fastest.
Arguments:
- signals: float32 [512, 32768], P('pt', 'tm'), may hold values from -6 to 6
- freq_bins: int32 [4], replicated, may hold values from 1 to 511
Outputs:
- cross_spectra: float32 [2, 4, 512, 512], P(None, None, 'pt', 'tm')
All inputs are finite; a program needn't handle non-finite values.
Results may differ from a plain program's by a relative error of at most 0.000064.
Values sent between devices are 32-bit elements; how exact they have to be, the bound alone decides.
No kernel may reach another device: no remote copies, remote signals or barrier semaphores. Data moves between devices by JAX's collectives and lax.ppermute only.
A program may use at most 64 MiB of HBM per device.

v0:
```python
import math
import jax
import jax.numpy as jnp
from jax import lax
from jax.sharding import PartitionSpec as P

SEGLEN = 1024
TWO_PI = 2.0 * math.pi


def shifted(value, axis, steps):
    count = lax.axis_size(axis)
    initial, last = (max(0, -steps), min(count, count - steps))
    return lax.ppermute(value, axis, [(source, source + steps) for source in range(initial, last)])


def dft_tables(freq_bins, seg_len):
    sample_index = jnp.arange(seg_len, dtype=jnp.int32)
    wrapped = sample_index[:, None] * freq_bins[None, :] % seg_len
    angles = wrapped.astype(jnp.float32) * (TWO_PI / seg_len)
    window = 0.5 - 0.5 * jnp.cos(sample_index.astype(jnp.float32) * (TWO_PI / seg_len))
    cosine = window[:, None] * jnp.cos(angles)
    sine_part = -window[:, None] * jnp.sin(angles)
    full_table = jnp.concatenate([cosine, sine_part], axis=1)
    half_len = seg_len // 2
    return jnp.concatenate([full_table[:half_len], full_table[half_len:]], axis=1)


def tile_products(left_side, right_side):
    stacked_right = jnp.concatenate([right_side[:, 0], right_side[:, 1]], axis=2)
    real_left = jnp.concatenate([left_side[:, 0], left_side[:, 1]], axis=2)
    imag_left = jnp.concatenate([left_side[:, 1], -left_side[:, 0]], axis=2)
    real_part = jnp.einsum(
        "fps,fqs->fpq", real_left, stacked_right, precision=lax.Precision.HIGHEST
    )
    imag_part = jnp.einsum(
        "fps,fqs->fpq", imag_left, stacked_right, precision=lax.Precision.HIGHEST
    )
    return jnp.stack([real_part, imag_part])


def body(signals, freq_bins):
    point_rows, sample_count = signals.shape
    half_len = SEGLEN // 2
    blocks_dev = sample_count // half_len
    bin_count = freq_bins.shape[0]
    columns = 2 * bin_count
    table = dft_tables(freq_bins, SEGLEN)
    blocks = signals.reshape(point_rows, blocks_dev, half_len)
    projected = jnp.einsum("pbn,nc->pbc", blocks, table, precision=lax.Precision.HIGHEST)
    incoming = shifted(signals[:, :half_len], "tm", -1)
    boundary = jnp.dot(
        incoming,
        table[:, columns:],
        precision=lax.Precision.HIGHEST,
        preferred_element_type=jnp.float32,
    )
    following = jnp.concatenate([projected[:, 1:, columns:], boundary[:, None, :]], axis=1)
    spectra = projected[:, :, :columns] + following
    is_last = lax.axis_index("tm") == lax.axis_size("tm") - 1
    segment_ids = jnp.arange(blocks_dev, dtype=jnp.int32)
    weight_mask = jnp.where(
        jnp.logical_and(is_last, segment_ids == blocks_dev - 1), 0.0, 1.0
    ).astype(jnp.float32)
    spectra = spectra * weight_mask[None, :, None]
    spectra_panel = spectra.reshape(point_rows, blocks_dev, 2, bin_count).transpose(3, 2, 0, 1)
    partial_tiles = tile_products(
        spectra_panel, lax.all_gather(spectra_panel, "pt", axis=2, tiled=True)
    )
    summed = lax.psum_scatter(partial_tiles, "tm", scatter_dimension=3, tiled=True)
    total_segments = blocks_dev * lax.axis_size("tm") - 1
    scale = 1.0 / (total_segments * 0.375 * SEGLEN)
    return summed * scale


def solution(mesh):
    in_specs = (P("pt", "tm"), P())
    out_specs = P(None, None, "pt", "tm")
    return jax.shard_map(body, mesh=mesh, in_specs=in_specs, out_specs=out_specs, check_vma=False)
```

profile of v0, /device:TPU:0, one launch (start us, length us, event | category | flops | bytes accessed | tf_op | source)
XLA Modules:
  0.0 97.8 jit_solution(1529557021851676892)
XLA Ops:
  6.5 0.0 reduce-scatter.2.cloned.1.call-start
  6.5 0.9 slice.33
  7.5 1.3 %collective-permute-start = (f32[64,512]{1,0:T(8,128)S(1)}, f32[64,512]{1,0:T(8,128)S(1)}, u32[]{:S(2)}, u32[]{:S(2)}) collective-permute-start(f32[64,512]{1,0:T(8,128)S(1)} %slice.33), channel_id=1, source_target_pairs={{1,0},{2,1},{3,2},{5,4},{6,5},{7,6},{9,8},{10,9},{11,10},{13,12},{... | collective-permute-start | bytes 393224 | tf_op jit(solution)/shard_map/ppermute | solution.py:14
  8.8 0.9 cosine_multiply_fusion
  9.7 4.2 %fusion.3 = f32[64,16,16]{0,2,1:T(8,128)S(1)} fusion(f32[8,16,8,512]{3,2,1,0:T(8,128)} %bitcast.33, f32[512,8]{0,1:T(8,128)S(1)} %get-tuple-element.10, f32[512,8]{0,1:T(8,128)S(1)} %get-tuple-element.9), kind=kOutput, calls=%fused_computation.5 | convolution fusion | flops 100671488 | bytes 2195456 | tf_op jit(solution)/shard_map/pbn,nc->pbc/dot_general | solution.py:50
  13.9 0.0 collective-permute-done
  13.9 0.2 convolution_bitcast_fusion.2
  14.1 0.1 fusion.6
  14.2 0.2 copy.7
  14.4 47.1 %all_gather.3 = f32[4,2,512,16]{3,0,1,2:T(4,128)S(1)} all-gather(f32[4,2,64,16]{3,0,1,2:T(4,128)S(1)} %copy.7), channel_id=1, replica_groups=mesh['pt'=8,'tm'=4] {'pt'}, dimensions={2}, use_global_device_ids=true | all-gather | bytes 294912 | tf_op jit(solution)/shard_map/all_gather | solution.py:68
  61.5 0.4 fusion.24
  61.9 0.3 copy.10
  62.2 0.3 copy.11
  62.5 0.6 convolution_bitcast_fusion.1
  63.2 0.6 convolution_bitcast_fusion
  63.8 1.0 %pad_maximum_fusion = f32[2,4,64,512]{3,2,1,0:T(8,128)} fusion(f32[1,4,64,512]{3,2,1,0:T(8,128)S(1)} %convolution_bitcast_fusion, f32[1,4,64,512]{3,2,1,0:T(8,128)S(1)} %convolution_bitcast_fusion.1), kind=kLoop, calls=%fused_computation.7 | loop fusion | flops 262144 | bytes 2097152 | tf_op jit(solution)/shard_map/stack | solution.py:39
  64.9 0.0 reduce-scatter.2.cloned.1.call-update
  64.9 24.3 %reduce-scatter.2.cloned.1.call-done = f32[2,4,64,128]{3,2,1,0:T(8,128)} async-done(((f32[2,4,64,512]{3,2,1,0:T(8,128)}), f32[2,4,64,128]{3,2,1,0:T(8,128)}) %reduce-scatter.2.cloned.1.call-update) | async-done | bytes 262160 | tf_op jit(solution)/shard_map/reduce_scatter | solution.py:70
  89.2 1.7 %broadcast_multiply_fusion = f32[2,4,64,128]{3,2,1,0:T(8,128)} fusion(f32[2,4,64,128]{3,2,1,0:T(8,128)} %reduce-scatter.2.cloned.1.call-done), kind=kLoop, calls=%fused_computation.9 | loop fusion | flops 65536 | bytes 524288 | tf_op jit(solution)/shard_map/mul | solution.py:73
  (7 shorter events, 0.1 us)
Async XLA Ops:
  6.5 82.7 %reduce-scatter.2.cloned.1.call-start = ((), (), s32[]{:S(2)}) async-start(), calls=%async_computation.1 | async-start | bytes 1310720 | tf_op jit(solution)/shard_map/reduce_scatter | solution.py:70
  7.5 6.4 %collective-permute-start = (f32[64,512]{1,0:T(8,128)S(1)}, f32[64,512]{1,0:T(8,128)S(1)}, u32[]{:S(2)}, u32[]{:S(2)}) collective-permute-start(f32[64,512]{1,0:T(8,128)S(1)} %slice.33), channel_id=1, source_target_pairs={{1,0},{2,1},{3,2},{5,4},{6,5},{7,6},{9,8},{10,9},{11,10},{13,12},{... | collective-permute-start | bytes 393224 | tf_op jit(solution)/shard_map/ppermute | solution.py:14
Sparse Core Ops, SparseCore 0:
  65.0 24.1 reduce-scatter.1
where the time goes:
time: 98 us; the launch traced here: 97.8 us
  blocking collectives  47.1 us (48%)
  waiting for transfers between devices  24.4 us (25%)
  between operations  13.5 us (14%)
  matrix products  5.6 us (6%)
  other arithmetic  3.79 us (4%)
  local copies, waits for them, and re-layouts  2.13 us (2%)
  starting transfers between devices  1.29 us (1%)
    all_gather x1, blocking collectives, body(): lax.all_gather(spectra_panel, 'pt', axis=2, tiled=True)  47.1 us
    reduce_scatter x1, waiting for transfers between devices, body(): lax.psum_scatter(partial_tiles, 'tm', scatter_dimension=3, tiled=True)  24.3 us
    dot_general x1, matrix products, body(): jnp.einsum('pbn,nc->pbc', blocks, table, precision=lax.Precision.HIGHEST)  4.15 us
  transfers between devices with their start and end apart: 2, of which 1 were waited for; matrix products, arithmetic and copies ran while one was open for 5% of the time, Pallas kernels for 0%

commit v1 on v0

--- a/solution.py
+++ b/solution.py
@@ -1,3 +1,4 @@
+import functools
 import math
 import jax
 import jax.numpy as jnp
@@ -6,6 +7,34 @@
 
 SEGLEN = 1024
 TWO_PI = 2.0 * math.pi
+
+
+def move_group(obj, dim_no):
+    obj = jnp.moveaxis(obj, 0, dim_no)
+    out_arr = obj.shape
+    return obj.reshape(
+        *out_arr[:dim_no], out_arr[dim_no] * out_arr[dim_no + 1], *out_arr[dim_no + 2 :]
+    )
+
+
+def roads_recover(values, ax_name):
+    w2, latest = (lax.axis_size(ax_name), lax.axis_index(ax_name))
+    before, near = (values[None], 1)
+    while near < w2:
+        back = lax.ppermute(before, ax_name, tuple(((q, q ^ near) for q in range(w2))))
+        carry_out = latest & near == 0
+        before = jnp.concatenate(
+            [jnp.where(carry_out, before, back), jnp.where(carry_out, back, before)]
+        )
+        near *= 2
+    return before
+
+
+def name_screen(chunk, inputs, ndim_at):
+    return move_group(roads_recover(chunk, inputs), ndim_at)
+
+
+guide_object_over_axis = functools.partial(name_screen, inputs="pt", ndim_at=2)
 
 
 def shifted(value, axis, steps):
@@ -64,9 +93,7 @@
     ).astype(jnp.float32)
     spectra = spectra * weight_mask[None, :, None]
     spectra_panel = spectra.reshape(point_rows, blocks_dev, 2, bin_count).transpose(3, 2, 0, 1)
-    partial_tiles = tile_products(
-        spectra_panel, lax.all_gather(spectra_panel, "pt", axis=2, tiled=True)
-    )
+    partial_tiles = tile_products(spectra_panel, guide_object_over_axis(spectra_panel))
     summed = lax.psum_scatter(partial_tiles, "tm", scatter_dimension=3, tiled=True)
     total_segments = blocks_dev * lax.axis_size("tm") - 1
     scale = 1.0 / (total_segments * 0.375 * SEGLEN)

time: 98 us -> 77.6 us (0.79)
  blocking collectives: 47.1 us -> 0 us
  waiting for transfers between devices: 24.4 us -> 43.4 us
  starting transfers between devices: 1.29 us -> 9.48 us
    all_gather x1 -> x0, blocking collectives: 47.1 us -> none  [body(): lax.all_gather(spectra_panel, 'pt', axis=2, tiled=True)]
    ppermute x0 -> x3, waiting for transfers between devices: none -> 17.9 us  [roads_recover(): lax.ppermute(before, ax_name, tuple(((q, q ^ near) for q in range(w2))))]
    ppermute x0 -> x3, starting transfers between devices: none -> 8.19 us  [roads_recover(): lax.ppermute(before, ax_name, tuple(((q, q ^ near) for q in range(w2))))]
    reduce_scatter x1, waiting for transfers between devices: 24.3 us -> 25.5 us  [body(): lax.psum_scatter(partial_tiles, 'tm', scatter_dimension=3, tiled=True)]
  transfers between devices with their start and end apart: 2 -> 5, of which waited for: 1 -> 4; matrix products, arithmetic and copies ran while one was open for 5% -> 7% of each run, Pallas kernels for 0% -> 0%
where the time goes in v1:
time: 77.6 us; the launch traced here: 77.4 us
  waiting for transfers between devices  43.4 us (56%)
  between operations  13.5 us (17%)
  starting transfers between devices  9.48 us (12%)
  matrix products  5.59 us (7%)
  other arithmetic  3.95 us (5%)
  local copies, waits for them, and re-layouts  1.41 us (2%)
    reduce_scatter x1, waiting for transfers between devices, body(): lax.psum_scatter(partial_tiles, 'tm', scatter_dimension=3, tiled=True)  25.5 us
    ppermute x3, waiting for transfers between devices, roads_recover(): lax.ppermute(before, ax_name, tuple(((q, q ^ near) for q in range(w2))))  17.9 us
    ppermute x3, starting transfers between devices, roads_recover(): lax.ppermute(before, ax_name, tuple(((q, q ^ near) for q in range(w2))))  8.19 us
    dot_general x1, matrix products, body(): jnp.einsum('pbn,nc->pbc', blocks, table, precision=lax.Precision.HIGHEST)  4.15 us
    mul x1, other arithmetic, body(): return summed * scale  1.68 us
  transfers between devices with their start and end apart: 5, of which 4 were waited for; matrix products, arithmetic and copies ran while one was open for 7% of the time, Pallas kernels for 0%

profile of v1, /device:TPU:0, one launch (start us, length us, event | category | flops | bytes accessed | tf_op | source)
XLA Modules:
  0.0 77.4 jit_solution(10008782146363431330)
XLA Ops:
  6.5 0.0 reduce-scatter.2.cloned.1.call-start
  6.5 0.9 %slice.33 = f32[64,512]{1,0:T(8,128)S(1)} slice(f32[64,8192]{1,0:T(8,128)} %param.2), slice={[0:64], [0:512]} | slice | bytes 262144 | tf_op jit(solution)/shard_map/slice | solution.py:80
  7.5 1.3 %collective-permute-start = (f32[64,512]{1,0:T(8,128)S(1)}, f32[64,512]{1,0:T(8,128)S(1)}, u32[]{:S(2)}, u32[]{:S(2)}) collective-permute-start(f32[64,512]{1,0:T(8,128)S(1)} %slice.33), channel_id=1, source_target_pairs={{1,0},{2,1},{3,2},{5,4},{6,5},{7,6},{9,8},{10,9},{11,10},{13,12},{... | collective-permute-start | bytes 393224 | tf_op jit(solution)/shard_map/ppermute | solution.py:43
  8.8 0.9 %cosine_multiply_fusion = (f32[1024,4]{0,1:T(4,128)S(1)}, f32[1024,4]{0,1:T(4,128)S(1)}) fusion(s32[4]{0:T(128)} %param.3, f32[1024]{0:T(1024)S(1)} %get-tuple-element.21, f32[1024]{0:T(1024)S(1)} %get-tuple-element.22), kind=kLoop, calls=%fused_computation.47 | loop fusion | flops 65536 | bytes 40976 | tf_op jit(solution)/shard_map/mul | solution.py:51
  9.7 4.2 %fusion.3 = f32[64,16,16]{0,2,1:T(8,128)S(1)} fusion(f32[8,16,8,512]{3,2,1,0:T(8,128)} %bitcast.48, f32[512,8]{0,1:T(8,128)S(1)} %get-tuple-element.18, f32[512,8]{0,1:T(8,128)S(1)} %get-tuple-element.17), kind=kOutput, calls=%fused_computation.5 | convolution fusion | flops 100671488 | bytes 2195456 | tf_op jit(solution)/shard_map/pbn,nc->pbc/dot_general | solution.py:79
  13.9 0.0 collective-permute-done
  13.9 0.2 convolution_bitcast_fusion.2
  14.1 0.1 fusion.6
  14.2 3.0 %collective-permute-start.1 = (f32[1,4,2,64,16]{3,4,1,2,0:T(8,128)S(1)}, f32[1,4,2,64,16]{3,4,1,2,0:T(8,128)S(1)}, u32[]{:S(2)}, u32[]{:S(2)}) collective-permute-start(f32[1,4,2,64,16]{3,4,1,2,0:T(8,128)S(1)} %bitcast.51), channel_id=1, source_target_pairs={{0,4},{4,0},{8,12},{12,8},{16,20},{20,16},{24,28},{28,24},{1,5},{5... | collective-permute-start | bytes 98312 | tf_op jit(solution)/shard_map/ppermute | solution.py:24
  17.3 2.6 %collective-permute-done.1 = f32[1,4,2,64,16]{3,4,1,2,0:T(8,128)S(1)} collective-permute-done((f32[1,4,2,64,16]{3,4,1,2,0:T(8,128)S(1)}, f32[1,4,2,64,16]{3,4,1,2,0:T(8,128)S(1)}, u32[]{:S(2)}, u32[]{:S(2)}) %collective-permute-start.1) | collective-permute-done | bytes 32800 | tf_op jit(solution)/shard_map/ppermute | solution.py:24
  19.9 2.3 %collective-permute-start.2 = (f32[2,4,2,64,16]{3,4,1,2,0:T(8,128)S(1)}, f32[2,4,2,64,16]{3,4,1,2,0:T(8,128)S(1)}, u32[]{:S(2)}, u32[]{:S(2)}) collective-permute-start(f32[2,4,2,64,16]{3,4,1,2,0:T(8,128)S(1)} %pad_maximum_fusion.5), channel_id=1, source_target_pairs={{0,8},{4,12},{8,0},{12,4},{16,24},{20,28},{24,16},{28,20},{1,9},{5... | collective-permute-start | bytes 196616 | tf_op jit(solution)/shard_map/ppermute | solution.py:24
  22.2 3.8 %collective-permute-done.2 = f32[2,4,2,64,16]{3,4,1,2,0:T(8,128)S(1)} collective-permute-done((f32[2,4,2,64,16]{3,4,1,2,0:T(8,128)S(1)}, f32[2,4,2,64,16]{3,4,1,2,0:T(8,128)S(1)}, u32[]{:S(2)}, u32[]{:S(2)}) %collective-permute-start.2) | collective-permute-done | bytes 65568 | tf_op jit(solution)/shard_map/ppermute | solution.py:24
  26.1 2.8 %collective-permute-start.3 = (f32[4,4,2,64,16]{3,4,1,2,0:T(8,128)S(1)}, f32[4,4,2,64,16]{3,4,1,2,0:T(8,128)S(1)}, u32[]{:S(2)}, u32[]{:S(2)}) collective-permute-start(f32[4,4,2,64,16]{3,4,1,2,0:T(8,128)S(1)} %pad_maximum_fusion.1), channel_id=1, source_target_pairs={{0,16},{4,20},{8,24},{12,28},{16,0},{20,4},{24,8},{28,12},{1,17},{... | collective-permute-start | bytes 393224 | tf_op jit(solution)/shard_map/ppermute | solution.py:24
  28.9 11.6 %collective-permute-done.3 = f32[4,4,2,64,16]{3,4,1,2,0:T(8,128)S(1)} collective-permute-done((f32[4,4,2,64,16]{3,4,1,2,0:T(8,128)S(1)}, f32[4,4,2,64,16]{3,4,1,2,0:T(8,128)S(1)}, u32[]{:S(2)}, u32[]{:S(2)}) %collective-permute-start.3) | collective-permute-done | bytes 131104 | tf_op jit(solution)/shard_map/ppermute | solution.py:24
  40.6 0.3 copy.5
  40.9 0.1 reshape.30
  41.1 0.6 convolution_bitcast_fusion
  41.7 0.6 convolution_bitcast_fusion.1
  42.3 1.0 %pad_maximum_fusion = f32[2,4,64,512]{3,2,1,0:T(8,128)} fusion(f32[1,4,64,512]{3,2,1,0:T(8,128)S(1)} %convolution_bitcast_fusion, f32[1,4,64,512]{3,2,1,0:T(8,128)S(1)} %convolution_bitcast_fusion.1), kind=kLoop, calls=%fused_computation.7 | loop fusion | flops 262144 | bytes 2097152 | tf_op jit(solution)/shard_map/stack | solution.py:68
  43.4 0.0 reduce-scatter.2.cloned.1.call-update
  43.4 25.5 %reduce-scatter.2.cloned.1.call-done = f32[2,4,64,128]{3,2,1,0:T(8,128)} async-done(((f32[2,4,64,512]{3,2,1,0:T(8,128)}), f32[2,4,64,128]{3,2,1,0:T(8,128)}) %reduce-scatter.2.cloned.1.call-update) | async-done | bytes 262160 | tf_op jit(solution)/shard_map/reduce_scatter | solution.py:97
  68.9 1.7 %broadcast_multiply_fusion = f32[2,4,64,128]{3,2,1,0:T(8,128)} fusion(f32[2,4,64,128]{3,2,1,0:T(8,128)} %reduce-scatter.2.cloned.1.call-done), kind=kLoop, calls=%fused_computation.14 | loop fusion | flops 65536 | bytes 524288 | tf_op jit(solution)/shard_map/mul | solution.py:100
  (14 shorter events, 0.3 us)
Async XLA Ops:
  6.5 62.4 %reduce-scatter.2.cloned.1.call-start = ((), (), s32[]{:S(2)}) async-start(), calls=%async_computation.1 | async-start | bytes 1310720 | tf_op jit(solution)/shard_map/reduce_scatter | solution.py:97
  7.5 6.4 %collective-permute-start = (f32[64,512]{1,0:T(8,128)S(1)}, f32[64,512]{1,0:T(8,128)S(1)}, u32[]{:S(2)}, u32[]{:S(2)}) collective-permute-start(f32[64,512]{1,0:T(8,128)S(1)} %slice.33), channel_id=1, source_target_pairs={{1,0},{2,1},{3,2},{5,4},{6,5},{7,6},{9,8},{10,9},{11,10},{13,12},{... | collective-permute-start | bytes 393224 | tf_op jit(solution)/shard_map/ppermute | solution.py:43
  14.2 5.6 %collective-permute-start.1 = (f32[1,4,2,64,16]{3,4,1,2,0:T(8,128)S(1)}, f32[1,4,2,64,16]{3,4,1,2,0:T(8,128)S(1)}, u32[]{:S(2)}, u32[]{:S(2)}) collective-permute-start(f32[1,4,2,64,16]{3,4,1,2,0:T(8,128)S(1)} %bitcast.51), channel_id=1, source_target_pairs={{0,4},{4,0},{8,12},{12,8},{16,20},{20,16},{24,28},{28,24},{1,5},{5... | collective-permute-start | bytes 98312 | tf_op jit(solution)/shard_map/ppermute | solution.py:24
  19.9 6.1 %collective-permute-start.2 = (f32[2,4,2,64,16]{3,4,1,2,0:T(8,128)S(1)}, f32[2,4,2,64,16]{3,4,1,2,0:T(8,128)S(1)}, u32[]{:S(2)}, u32[]{:S(2)}) collective-permute-start(f32[2,4,2,64,16]{3,4,1,2,0:T(8,128)S(1)} %pad_maximum_fusion.5), channel_id=1, source_target_pairs={{0,8},{4,12},{8,0},{12,4},{16,24},{20,28},{24,16},{28,20},{1,9},{5... | collective-permute-start | bytes 196616 | tf_op jit(solution)/shard_map/ppermute | solution.py:24
  26.1 14.4 %collective-permute-start.3 = (f32[4,4,2,64,16]{3,4,1,2,0:T(8,128)S(1)}, f32[4,4,2,64,16]{3,4,1,2,0:T(8,128)S(1)}, u32[]{:S(2)}, u32[]{:S(2)}) collective-permute-start(f32[4,4,2,64,16]{3,4,1,2,0:T(8,128)S(1)} %pad_maximum_fusion.1), channel_id=1, source_target_pairs={{0,16},{4,20},{8,24},{12,28},{16,0},{20,4},{24,8},{28,12},{1,17},{... | collective-permute-start | bytes 393224 | tf_op jit(solution)/shard_map/ppermute | solution.py:24
Sparse Core Ops, SparseCore 0:
  43.5 25.3 reduce-scatter.1
